TPU v7x, 32 devices: a whole 2x2x4 slice. The times are simulated.
32 devices in a mesh: fsdp: 4 (over x, core), tp: 8 (over z, y).
Axes of the slice: x: 2, y: 2, z: 4, core: 2. Of those that a mesh axis runs over, the one named last changes fastest.
Arguments:
- hidden_in: bfloat16 [8, 1024, 1024], P('fsdp', 'tp'), may hold values from -6 to 6
- grad_out: bfloat16 [8, 1024, 1024], P('fsdp', 'tp'), may hold values from -6 to 6
- condition: float32 [8, 1024], P('fsdp', 'tp'), may hold values from -6 to 6
- w_mod: bfloat16 [1024, 6144], P('tp', 'fsdp'), may hold values from -0.1875 to 0.1875
- b_mod: bfloat16 [6144], P('fsdp'), may hold values from -3 to 3
- w_qkv: bfloat16 [1024, 16, 192], P('fsdp', 'tp'), may hold values from -0.1875 to 0.1875
- b_qv: bfloat16 [16, 128], P('tp', 'fsdp'), may hold values from -2 to 2
- w_proj: bfloat16 [1024, 1024], P('tp', 'fsdp'), may hold values from -2 to 2
- b_proj: bfloat16 [1024], P('fsdp'), may hold values from -3 to 3
- w_fc1: bfloat16 [1024, 4096], P('fsdp', 'tp'), may hold values from -0.1875 to 0.1875
- b_fc1: bfloat16 [4096], P(('tp', 'fsdp')), may hold values from -3 to 3
- w_fc2: bfloat16 [4096, 1024], P('tp', 'fsdp'), may hold values from -0.375 to 0.375
- b_fc2: bfloat16 [1024], P('fsdp'), may hold values from -3 to 3
Outputs:
- block_out: float32 [8, 1024, 1024], P('fsdp', 'tp')
- grad_input: float32 [8, 1024, 1024], P('fsdp', 'tp')
- grad_cond: float32 [8, 1024], P('fsdp', 'tp')
- grad_w_mod: float32 [1024, 6144], P('tp', 'fsdp')
- grad_b_mod: float32 [6144], P('fsdp')
- grad_w_qkv: float32 [1024, 16, 192], P('fsdp', 'tp')
- grad_b_qv: float32 [16, 128], P('tp', 'fsdp')
- grad_w_proj: float32 [1024, 1024], P('tp', 'fsdp')
- grad_b_proj: float32 [1024], P('fsdp')
- grad_w_fc1: float32 [1024, 4096], P('fsdp', 'tp')
- grad_b_fc1: float32 [4096], P(('tp', 'fsdp'))
- grad_w_fc2: float32 [4096, 1024], P('tp', 'fsdp')
- grad_b_fc2: float32 [1024], P('fsdp')
All inputs are finite; a program needn't handle non-finite values.
Results may differ from a plain program's by a relative error of at most 0.013.
The roundings to bfloat16 on the way count: a program that leaves them out, or rounds other values in their place, can miss the bound.
Values may be sent and summed in bfloat16 or wider, within the bound.
No kernel may reach another device: no remote copies, remote signals or barrier semaphores. Data moves between devices by JAX's collectives and lax.ppermute only.
A program may use at most 128 MiB of HBM per device.

v0:
```python
import jax
import jax.numpy as jnp
from jax import lax
from jax.sharding import PartitionSpec as P

EPSILON = 1e-06


def layer_norm(values):
    center_mean = jnp.mean(values, -1, keepdims=True)
    centered = values - center_mean
    variance = jnp.mean(centered * centered, -1, keepdims=True)
    inv_std = lax.rsqrt(variance + EPSILON)
    return (centered * inv_std, inv_std)


def norm_back(grad_normed, normed, inv_std):
    return inv_std * (
        grad_normed
        - jnp.mean(grad_normed, -1, keepdims=True)
        - normed * jnp.mean(grad_normed * normed, -1, keepdims=True)
    )


def gelu_tanh(values):
    return jax.nn.gelu(values, approximate=True)


def piece_of(modulation, index, width):
    return modulation[:, None, index * width : (index + 1) * width]


def attend_one(items):
    query_rows, key_rows, value_rows = items
    score_scale = query_rows.shape[-1] ** (-0.5)
    scores = (
        jnp.einsum("qhe,khe->hqk", query_rows, key_rows, preferred_element_type=jnp.float32)
        * score_scale
    )
    row_max = jnp.max(scores, -1, keepdims=True)
    log_total = row_max + jnp.log(jnp.sum(jnp.exp(scores - row_max), -1, keepdims=True))
    probs_low = jnp.exp(scores - log_total).astype(jnp.bfloat16)
    attended = jnp.einsum("hqk,khe->qhe", probs_low, value_rows, preferred_element_type=jnp.float32)
    return (attended.astype(jnp.bfloat16), log_total)


def attend_back(items):
    query_rows, key_rows, value_rows, log_total, grad_attended = items
    score_scale = query_rows.shape[-1] ** (-0.5)
    scores = (
        jnp.einsum("qhe,khe->hqk", query_rows, key_rows, preferred_element_type=jnp.float32)
        * score_scale
    )
    probs = jnp.exp(scores - log_total)
    probs_low = probs.astype(jnp.bfloat16)
    grad_probs = jnp.einsum(
        "qhe,khe->hqk", grad_attended, value_rows, preferred_element_type=jnp.float32
    )
    inner = jnp.sum(probs * grad_probs, -1, keepdims=True)
    grad_scores = (probs * (grad_probs - inner)).astype(jnp.bfloat16)
    grad_query = (
        jnp.einsum("hqk,khe->qhe", grad_scores, key_rows, preferred_element_type=jnp.float32)
        * score_scale
    )
    grad_keys = (
        jnp.einsum("hqk,qhe->khe", grad_scores, query_rows, preferred_element_type=jnp.float32)
        * score_scale
    )
    grad_values = jnp.einsum(
        "hqk,qhe->khe", probs_low, grad_attended, preferred_element_type=jnp.float32
    )
    return jnp.concatenate([grad_query, grad_keys, grad_values], -1).astype(jnp.bfloat16)


def on_device(
    hidden_in,
    grad_out,
    condition,
    w_mod,
    b_mod,
    w_qkv,
    b_qv,
    w_proj,
    b_proj,
    w_fc1,
    b_fc1,
    w_fc2,
    b_fc2,
):
    latents = hidden_in.shape[0]
    width = hidden_in.shape[2]
    (
        mod_rows,
        mod_bias,
        qkv_cols,
        qv_bias,
        proj_rows,
        proj_bias,
        fc1_cols,
        fc1_bias,
        fc2_rows,
        fc2_bias,
    ) = (
        lax.all_gather(w_mod, "fsdp", axis=1, tiled=True),
        lax.all_gather(b_mod, "fsdp", axis=0, tiled=True),
        lax.all_gather(w_qkv, "fsdp", axis=0, tiled=True),
        lax.all_gather(b_qv, "fsdp", axis=1, tiled=True),
        lax.all_gather(w_proj, "fsdp", axis=1, tiled=True),
        lax.all_gather(b_proj, "fsdp", axis=0, tiled=True),
        lax.all_gather(w_fc1, "fsdp", axis=0, tiled=True),
        lax.all_gather(b_fc1, "fsdp", axis=0, tiled=True),
        lax.all_gather(w_fc2, "fsdp", axis=1, tiled=True),
        lax.all_gather(b_fc2, "fsdp", axis=0, tiled=True),
    )
    heads_here = qkv_cols.shape[1]
    head_dim = qkv_cols.shape[2] // 3
    cond_act, silu_back = jax.vjp(jax.nn.silu, condition)
    cond_low = cond_act.astype(jnp.bfloat16)
    modulation = lax.psum(
        jnp.dot(cond_low, mod_rows, preferred_element_type=jnp.float32), "tp"
    ) + mod_bias.astype(jnp.float32)
    shift_one = piece_of(modulation, 0, width)
    scale_one = piece_of(modulation, 1, width)
    gate_one = piece_of(modulation, 2, width)
    shift_two = piece_of(modulation, 3, width)
    scale_two = piece_of(modulation, 4, width)
    gate_two = piece_of(modulation, 5, width)
    resid_in = hidden_in.astype(jnp.float32)
    normed_one, inv_one = layer_norm(resid_in)
    attn_local = (normed_one * (1.0 + scale_one) + shift_one).astype(jnp.bfloat16)
    attn_rows = lax.all_gather(attn_local, "tp", axis=1, tiled=True)
    seq_len = attn_rows.shape[1]
    total_rows = latents * seq_len
    qkv_matrix = qkv_cols.reshape(width, heads_here * 3 * head_dim)
    qv_float = qv_bias.astype(jnp.float32)
    bias_three = jnp.concatenate(
        [
            qv_float[:, :head_dim],
            jnp.zeros((heads_here, head_dim), jnp.float32),
            qv_float[:, head_dim:],
        ],
        -1,
    )
    projected = (
        jnp.dot(
            attn_rows.reshape(total_rows, width), qkv_matrix, preferred_element_type=jnp.float32
        ).reshape(latents, seq_len, heads_here, 3 * head_dim)
        + bias_three
    ).astype(jnp.bfloat16)
    query_rows = projected[..., :head_dim]
    key_rows = projected[..., head_dim : 2 * head_dim]
    value_rows = projected[..., 2 * head_dim :]
    attended, log_total = lax.map(attend_one, (query_rows, key_rows, value_rows))
    attended_flat = attended.reshape(total_rows, heads_here * head_dim)
    attn_terms = jnp.dot(attended_flat, proj_rows, preferred_element_type=jnp.float32).reshape(
        latents, seq_len, width
    )
    attn_sums = lax.psum_scatter(attn_terms, "tp", scatter_dimension=1, tiled=True)
    attn_branch = attn_sums + proj_bias.astype(jnp.float32)
    resid_mid = resid_in + gate_one * attn_branch
    normed_two, inv_two = layer_norm(resid_mid)
    mlp_local = (normed_two * (1.0 + scale_two) + shift_two).astype(jnp.bfloat16)
    mlp_rows = lax.all_gather(mlp_local, "tp", axis=1, tiled=True)
    pre_act = jnp.dot(
        mlp_rows.reshape(total_rows, width), fc1_cols, preferred_element_type=jnp.float32
    ) + fc1_bias.astype(jnp.float32)
    act_float, gelu_back = jax.vjp(gelu_tanh, pre_act)
    act_low = act_float.astype(jnp.bfloat16)
    mlp_terms = jnp.dot(act_low, fc2_rows, preferred_element_type=jnp.float32).reshape(
        latents, seq_len, width
    )
    mlp_branch = lax.psum_scatter(
        mlp_terms, "tp", scatter_dimension=1, tiled=True
    ) + fc2_bias.astype(jnp.float32)
    block_out = resid_mid + gate_two * mlp_branch
    cotangent = grad_out.astype(jnp.float32)
    grad_gate_two = jnp.sum(cotangent * mlp_branch, 1)
    grad_mlp_out = (gate_two * cotangent).astype(jnp.bfloat16)
    grad_mlp_rows = lax.all_gather(grad_mlp_out, "tp", axis=1, tiled=True).reshape(
        total_rows, width
    )
    grad_fc2 = jnp.dot(act_low.T, grad_mlp_rows, preferred_element_type=jnp.float32)
    grad_fc2_bias = jnp.sum(grad_mlp_rows.astype(jnp.float32), 0)
    grad_act = jnp.dot(grad_mlp_rows, fc2_rows.T, preferred_element_type=jnp.float32)
    grad_pre = gelu_back(grad_act)[0].astype(jnp.bfloat16)
    grad_fc1 = jnp.dot(
        mlp_rows.reshape(total_rows, width).T, grad_pre, preferred_element_type=jnp.float32
    )
    grad_fc1_bias = jnp.sum(grad_pre.astype(jnp.float32), 0)
    mlp_in_terms = jnp.dot(grad_pre, fc1_cols.T, preferred_element_type=jnp.float32).reshape(
        latents, seq_len, width
    )
    grad_mlp_in = lax.psum_scatter(mlp_in_terms, "tp", scatter_dimension=1, tiled=True)
    grad_scale_two = jnp.sum(grad_mlp_in * normed_two, 1)
    grad_shift_two = jnp.sum(grad_mlp_in, 1)
    grad_mid = cotangent + norm_back(grad_mlp_in * (1.0 + scale_two), normed_two, inv_two)
    grad_gate_one = jnp.sum(grad_mid * attn_branch, 1)
    grad_attn_out = (gate_one * grad_mid).astype(jnp.bfloat16)
    grad_attn_rows = lax.all_gather(grad_attn_out, "tp", axis=1, tiled=True).reshape(
        total_rows, width
    )
    grad_proj = jnp.dot(attended_flat.T, grad_attn_rows, preferred_element_type=jnp.float32)
    grad_proj_bias = jnp.sum(grad_attn_rows.astype(jnp.float32), 0)
    grad_attended = (
        jnp.dot(grad_attn_rows, proj_rows.T, preferred_element_type=jnp.float32)
        .astype(jnp.bfloat16)
        .reshape(latents, seq_len, heads_here, head_dim)
    )
    grad_projected = lax.map(
        attend_back, (query_rows, key_rows, value_rows, log_total, grad_attended)
    )
    grad_flat = grad_projected.reshape(total_rows, heads_here * 3 * head_dim)
    grad_qkv = jnp.dot(
        attn_rows.reshape(total_rows, width).T, grad_flat, preferred_element_type=jnp.float32
    ).reshape(width, heads_here, 3 * head_dim)
    bias_sums = jnp.sum(grad_projected.astype(jnp.float32), (0, 1))
    grad_qv_bias = jnp.concatenate([bias_sums[:, :head_dim], bias_sums[:, 2 * head_dim :]], -1)
    attn_in_terms = jnp.dot(grad_flat, qkv_matrix.T, preferred_element_type=jnp.float32).reshape(
        latents, seq_len, width
    )
    grad_attn_in = lax.psum_scatter(attn_in_terms, "tp", scatter_dimension=1, tiled=True)
    grad_scale_one = jnp.sum(grad_attn_in * normed_one, 1)
    grad_shift_one = jnp.sum(grad_attn_in, 1)
    grad_input = grad_mid + norm_back(grad_attn_in * (1.0 + scale_one), normed_one, inv_one)
    mod_terms = jnp.concatenate(
        [
            grad_shift_one,
            grad_scale_one,
            grad_gate_one,
            grad_shift_two,
            grad_scale_two,
            grad_gate_two,
        ],
        -1,
    )
    grad_modulation = lax.psum(mod_terms, "tp")
    grad_mod_low = grad_modulation.astype(jnp.bfloat16)
    grad_mod_w = jnp.dot(cond_low.T, grad_mod_low, preferred_element_type=jnp.float32)
    grad_mod_bias = jnp.sum(grad_modulation, 0)
    grad_cond = silu_back(jnp.dot(grad_mod_low, mod_rows.T, preferred_element_type=jnp.float32))[0]
    owned = (
        lax.psum_scatter(grad_mod_w, "fsdp", scatter_dimension=1, tiled=True),
        lax.psum_scatter(grad_mod_bias, "fsdp", scatter_dimension=0, tiled=True),
        lax.psum_scatter(grad_qkv, "fsdp", scatter_dimension=0, tiled=True),
        lax.psum_scatter(grad_qv_bias, "fsdp", scatter_dimension=1, tiled=True),
        lax.psum_scatter(grad_proj, "fsdp", scatter_dimension=1, tiled=True),
        lax.psum_scatter(grad_proj_bias, "fsdp", scatter_dimension=0, tiled=True),
        lax.psum_scatter(grad_fc1, "fsdp", scatter_dimension=0, tiled=True),
        lax.psum_scatter(grad_fc1_bias, "fsdp", scatter_dimension=0, tiled=True),
        lax.psum_scatter(grad_fc2, "fsdp", scatter_dimension=1, tiled=True),
        lax.psum_scatter(grad_fc2_bias, "fsdp", scatter_dimension=0, tiled=True),
    )
    return (
        block_out,
        grad_input,
        grad_cond,
        owned[0],
        owned[1],
        owned[2],
        owned[3],
        owned[4],
        owned[5],
        owned[6],
        owned[7],
        owned[8],
        owned[9],
    )


def solution(mesh):
    placed = (
        P("fsdp", "tp", None),
        P("fsdp", "tp", None),
        P("fsdp", "tp"),
        P("tp", "fsdp"),
        P("fsdp"),
        P("fsdp", "tp", None),
        P("tp", "fsdp"),
        P("tp", "fsdp"),
        P("fsdp"),
        P("fsdp", "tp"),
        P(("tp", "fsdp")),
        P("tp", "fsdp"),
        P("fsdp"),
    )
    return jax.shard_map(
        on_device,
        mesh=mesh,
        in_specs=placed,
        out_specs=(
            P("fsdp", "tp", None),
            P("fsdp", "tp", None),
            P("fsdp", "tp"),
            P("tp", "fsdp"),
            P("fsdp"),
            P("fsdp", "tp", None),
            P("tp", "fsdp"),
            P("tp", "fsdp"),
            P("fsdp"),
            P("fsdp", "tp"),
            P(("tp", "fsdp")),
            P("tp", "fsdp"),
            P("fsdp"),
        ),
        check_vma=False,
    )
```

profile of v0, /device:TPU:0, one launch (start us, length us, event | category | flops | bytes accessed | tf_op | source)
XLA Modules:
  0.0 1253.0 jit_solution(13203060806068812908)
XLA Ops:
  8.7 6.2 all-gather
  17.5 14.5 %all-gather.13.cloned.1.call-done = bf16[128,6144]{1,0:T(8,128)(2,1)} async-done(((bf16[128,1536]{1,0:T(8,128)(2,1)}), bf16[128,6144]{1,0:T(8,128)(2,1)}) %all-gather.13.cloned.1.call-update) | async-done | bytes 1572880 | tf_op jit(solution)/shard_map/all_gather | solution.py:104
  32.0 1.7 fusion.88
  33.7 37.5 %psum.14 = f32[2,6144]{1,0:T(2,128)S(1)} all-reduce(f32[2,6144]{1,0:T(2,128)S(1)} %fusion.88), channel_id=1, replica_groups=mesh['fsdp'=4,'tp'=8] {'tp'}, use_global_device_ids=true, to_apply=%region_0.1 | all-reduce | flops 12288 | bytes 98304 | tf_op jit(solution)/shard_map/psum | solution.py:119
  71.9 2.1 fusion.67
  74.1 5.1 all-gather.1
  79.4 5.8 all_gather.47
  85.3 8.7 all_gather.45
  94.0 49.3 %all-gather.15.cloned.1.call-done = bf16[2,1024,1024]{2,1,0:T(8,128)(2,1)} async-done(((bf16[2,128,1024]{2,1,0:T(8,128)(2,1)}), bf16[2,1024,1024]{2,1,0:T(8,128)(2,1)}) %all-gather.15.cloned.1.call-update) | async-done | bytes 4194320 | tf_op jit(solution)/shard_map/all_gather | solution.py:131
  143.3 4.0 add_convert_fusion
  147.5 8.6 while.22
  148.8 1.4 exponential_reduce_fusion.2
  150.2 1.5 fusion.139
  153.1 1.4 exponential_reduce_fusion.2
  154.5 1.5 fusion.139
  156.0 4.5 fusion.78
  161.2 5.1 all-gather.2
  166.3 140.4 %reduce-scatter.13.cloned.1.call-done = f32[2,128,1024]{2,1,0:T(8,128)} async-done(((f32[2,1024,1024]{2,1,0:T(8,128)}), f32[2,128,1024]{2,1,0:T(8,128)}) %reduce-scatter.13.cloned.1.call-update) | async-done | bytes 1048592 | tf_op jit(solution)/shard_map/reduce_scatter | solution.py:158
  306.7 1.5 fusion.92
  310.2 2.0 fusion.74
  312.2 5.2 all-gather.3
  317.5 6.5 all-gather.19.cloned.1.call-done
  323.9 75.4 %all-gather.17.cloned.1.call-done = bf16[2,1024,1024]{2,1,0:T(8,128)(2,1)} async-done(((bf16[2,128,1024]{2,1,0:T(8,128)(2,1)}), bf16[2,1024,1024]{2,1,0:T(8,128)(2,1)}) %all-gather.17.cloned.1.call-update) | async-done | bytes 4194320 | tf_op jit(solution)/shard_map/all_gather | solution.py:163
  399.4 6.8 fusion.97
  406.1 10.0 all-gather.21.cloned.1.call-done
  416.2 75.6 %all-gather.23.cloned.1.call-done = bf16[2,1024,1024]{2,1,0:T(8,128)(2,1)} async-done(((bf16[2,128,1024]{2,1,0:T(8,128)(2,1)}), bf16[2,1024,1024]{2,1,0:T(8,128)(2,1)}) %all-gather.23.cloned.1.call-update) | async-done | bytes 4194320 | tf_op jit(solution)/shard_map/all_gather | solution.py:179
  491.7 9.0 convert_reduce_fusion.2
  500.7 5.6 fusion.98
  506.4 8.6 fusion.90
  515.6 5.1 all-gather.4
  520.7 131.8 %reduce-scatter.17.cloned.1.call-done = f32[2,128,1024]{2,1,0:T(8,128)} async-done(((f32[2,1024,1024]{2,1,0:T(8,128)}), f32[2,128,1024]{2,1,0:T(8,128)}) %reduce-scatter.17.cloned.1.call-update) | async-done | bytes 1048592 | tf_op jit(solution)/shard_map/reduce_scatter | solution.py:193
  652.5 1.7 multiply_reduce_fusion.2
  654.3 148.5 %reduce-scatter.15.cloned.1.call-done = f32[2,128,1024]{2,1,0:T(8,128)} async-done(((f32[2,1024,1024]{2,1,0:T(8,128)}), f32[2,128,1024]{2,1,0:T(8,128)}) %reduce-scatter.15.cloned.1.call-update) | async-done | bytes 1048592 | tf_op jit(solution)/shard_map/reduce_scatter | solution.py:172
  802.8 3.6 fusion.75
  808.3 72.0 %all-gather.25.cloned.1.call-done = bf16[2,1024,1024]{2,1,0:T(8,128)(2,1)} async-done(((bf16[2,128,1024]{2,1,0:T(8,128)(2,1)}), bf16[2,1024,1024]{2,1,0:T(8,128)(2,1)}) %all-gather.25.cloned.1.call-update) | async-done | bytes 4194320 | tf_op jit(solution)/shard_map/all_gather | solution.py:199
  880.3 3.4 convolution_convert_fusion
  884.9 21.7 %while.23 = (s32[]{:T(128)}, bf16[2,1024,2,192]{1,3,2,0:T(8,128)(2,1)}, bf16[2,1024,2,64]{1,3,2,0:T(8,128)(2,1)S(1)}, bf16[2,1024,2,64]{1,3,2,0:T(8,128)(2,1)S(1...) while((s32[]{:T(128)}, ...), condition=%wide.region_16.17_spmd, body=%wide.region_14.16_spmd.sunk | while | flops 1370355712 | bytes 79751328 | solution.py:209
  886.2 1.6 fusion.149
  887.8 2.0 multiply_reduce_fusion.11
  889.8 2.4 multiply_convert_fusion.9
  893.1 1.4 fusion.150
  897.1 1.6 fusion.149
  898.6 2.0 multiply_reduce_fusion.11
  900.6 2.4 multiply_convert_fusion.9
  903.9 1.4 fusion.150
  906.6 7.0 convolution_bitcast_fusion
  913.7 1.3 copy-done.8
  916.6 6.6 fusion.101
  923.3 7.3 fusion.89
  931.4 3.8 fusion.100
  935.3 1.6 copy.70
  937.6 3.0 fusion.99
  940.6 119.2 %reduce-scatter.19.cloned.1.call-done = f32[2,128,1024]{2,1,0:T(8,128)} async-done(((f32[2,1024,1024]{2,1,0:T(8,128)}), f32[2,128,1024]{2,1,0:T(8,128)}) %reduce-scatter.19.cloned.1.call-update) | async-done | bytes 1048592 | tf_op jit(solution)/shard_map/reduce_scatter | solution.py:221
  1059.8 1.8 fusion.72
  1061.7 35.9 %psum.15 = f32[2,6144]{1,0:T(2,128)S(1)} all-reduce(f32[2,6144]{1,0:T(2,128)S(1)} %constant_dynamic-update-slice_fusion), channel_id=1, replica_groups=mesh['fsdp'=4,'tp'=8] {'tp'}, use_global_device_ids=true, to_apply=%region_26.27 | all-reduce | flops 12288 | bytes 98304 | tf_op jit(solution)/shard_map/psum | solution.py:236
  1097.5 2.3 fusion.80
  1102.4 3.0 convert_reduce_fusion
  1106.6 1.4 copy.82
  1108.0 11.3 all-reduce.4
  1122.9 2.6 fusion.71
  1125.5 24.4 %reduce-scatter.29.cloned.1.call-done = f32[512,256]{1,0:T(8,128)} async-done(((f32[512,1024]{1,0:T(8,128)}), f32[512,256]{1,0:T(8,128)}) %reduce-scatter.29.cloned.1.call-update) | async-done | bytes 524304 | tf_op jit(solution)/shard_map/reduce_scatter | solution.py:250
  1149.9 24.6 %reduce-scatter.25.cloned.1.call-done = f32[128,256]{1,0:T(8,128)} async-done(((f32[128,1024]{1,0:T(8,128)}), f32[128,256]{1,0:T(8,128)}) %reduce-scatter.25.cloned.1.call-update) | async-done | bytes 131088 | tf_op jit(solution)/shard_map/reduce_scatter | solution.py:246
  1174.5 31.1 %reduce-scatter.23.cloned.1.call-done = f32[256,2,192]{0,2,1:T(8,128)} async-done(((f32[1024,2,192]{0,2,1:T(8,128)}), f32[256,2,192]{0,2,1:T(8,128)}) %reduce-scatter.23.cloned.1.call-update) | async-done | bytes 393232 | tf_op jit(solution)/shard_map/reduce_scatter | solution.py:244
  1205.5 40.8 %reduce-scatter.21.cloned.1.call-done = f32[128,1536]{1,0:T(8,128)} async-done(((f32[128,6144]{1,0:T(8,128)}), f32[128,1536]{1,0:T(8,128)}) %reduce-scatter.21.cloned.1.call-update) | async-done | bytes 786448 | tf_op jit(solution)/shard_map/reduce_scatter | solution.py:242
  (167 shorter events, 29.6 us)
Async XLA Ops:
  7.2 67.0 %copy-start.24 = (bf16[2,32]{1,0:T(2,128)(2,1)S(1)}, bf16[2,32]{1,0:T(2,128)(2,1)}, u32[]{:S(2)}) copy-start(bf16[2,32]{1,0:T(2,128)(2,1)} %param.23) | copy-start | bytes 388
  7.2 72.2 %copy-start.18 = (bf16[128,256]{1,0:T(8,128)(2,1)S(1)}, bf16[128,256]{1,0:T(8,128)(2,1)}, u32[]{:S(2)}) copy-start(bf16[128,256]{1,0:T(8,128)(2,1)} %param.24) | copy-start | bytes 196612
  7.2 78.1 %copy-start.15 = (bf16[256,2,192]{0,2,1:T(8,128)(2,1)S(1)}, bf16[256,2,192]{0,2,1:T(8,128)(2,1)}, u32[]{:S(2)}) copy-start(bf16[256,2,192]{0,2,1:T(8,128)(2,1)} %param.22) | copy-start | bytes 589828
  7.2 24.8 %all-gather.13.cloned.1.call-start = ((), (), s32[]{:S(2)}) async-start(), calls=%async_computation.10 | async-start | bytes 1966080 | tf_op jit(solution)/shard_map/all_gather | solution.py:104
  7.9 135.4 %all-gather.15.cloned.1.call-start = ((), (), s32[]{:S(2)}) async-start(), calls=%async_computation.11 | async-start | bytes 4718592 | tf_op jit(solution)/shard_map/all_gather | solution.py:131
  16.1 131.2 %copy-start.19 = (f32[2,128]{1,0:T(2,128)}, f32[2,128]{1,0:T(2,128)S(1)}, u32[]{:S(2)}) copy-start(f32[2,128]{1,0:T(2,128)S(1)} %broadcast_multiply_fusion.5) | copy-start | bytes 3076
  17.5 56.6 %copy-start.21 = (f32[2,128]{1,0:T(2,128)}, f32[2,128]{1,0:T(2,128)S(1)}, u32[]{:S(2)}) copy-start(f32[2,128]{1,0:T(2,128)S(1)} %add_rsqrt_fusion.1) | copy-start | bytes 3076
  71.3 0.6 copy-start.16
  74.1 232.6 %reduce-scatter.13.cloned.1.call-start = ((), (), s32[]{:S(2)}) async-start(), calls=%async_computation.12 | async-start | bytes 9437184 | tf_op jit(solution)/shard_map/reduce_scatter | solution.py:158
  94.0 53.3 %copy-start.13 = (bf16[1024,2,192]{0,2,1:T(8,128)(2,1)}, bf16[1024,2,192]{0,2,1:T(8,128)(2,1)S(1)}, u32[]{:S(2)}) copy-start(bf16[1024,2,192]{0,2,1:T(8,128)(2,1)S(1)} %all_gather.45) | copy-start | bytes 2359300
  156.0 4.5 copy-start.10
  160.6 0.7 copy-start.28
  160.6 146.1 %copy-start = (bf16[2,128,1024]{2,1,0:T(8,128)(2,1)S(1)}, bf16[2,128,1024]{2,1,0:T(8,128)(2,1)}, u32[]{:S(2)}) copy-start(bf16[2,128,1024]{2,1,0:T(8,128)(2,1)} %param.17) | copy-start | bytes 1572868
  160.6 151.6 %copy-start.25 = (bf16[128]{0:T(256)(128)(2,1)S(1)}, bf16[128]{0:T(256)(128)(2,1)}, u32[]{:S(2)}) copy-start(bf16[128]{0:T(256)(128)(2,1)} %param.27) | copy-start | bytes 772
  160.6 163.4 %all-gather.19.cloned.1.call-start = ((), (), s32[]{:S(2)}) async-start(), calls=%async_computation.14 | async-start | bytes 1310720 | tf_op jit(solution)/shard_map/all_gather | solution.py:110
  161.2 238.2 %all-gather.17.cloned.1.call-start = ((), (), s32[]{:S(2)}) async-start(), calls=%async_computation.13 | async-start | bytes 4718592 | tf_op jit(solution)/shard_map/all_gather | solution.py:163
  309.5 106.6 %all-gather.21.cloned.1.call-start = ((), (), s32[]{:S(2)}) async-start(), calls=%async_computation.15 | async-start | bytes 1310720 | tf_op jit(solution)/shard_map/all_gather | solution.py:112
  310.1 181.6 %all-gather.23.cloned.1.call-start = ((), (), s32[]{:S(2)}) async-start(), calls=%async_computation.17 | async-start | bytes 4718592 | tf_op jit(solution)/shard_map/all_gather | solution.py:179
  312.2 340.4 %reduce-scatter.17.cloned.1.call-start = ((), (), s32[]{:S(2)}) async-start(), calls=%async_computation.18 | async-start | bytes 9437184 | tf_op jit(solution)/shard_map/reduce_scatter | solution.py:193
  491.7 9.0 copy-start.27
  500.7 5.6 copy-start.12
  506.4 296.4 %reduce-scatter.15.cloned.1.call-start = ((), (), s32[]{:S(2)}) async-start(), calls=%async_computation.16 | async-start | bytes 9437184 | tf_op jit(solution)/shard_map/reduce_scatter | solution.py:172
  515.0 0.7 copy-start.29
  515.0 287.8 %copy-start.9 = (bf16[2,128,1024]{2,1,0:T(8,128)(2,1)S(1)}, bf16[2,128,1024]{2,1,0:T(8,128)(2,1)}, u32[]{:S(2)}) copy-start(bf16[2,128,1024]{2,1,0:T(8,128)(2,1)} %param.18) | copy-start | bytes 1572868
  515.0 365.3 %all-gather.25.cloned.1.call-start = ((), (), s32[]{:S(2)}) async-start(), calls=%async_computation.19 | async-start | bytes 4718592 | tf_op jit(solution)/shard_map/all_gather | solution.py:199
  806.4 1.0 copy-start.3
  808.2 251.5 %reduce-scatter.19.cloned.1.call-start = ((), (), s32[]{:S(2)}) async-start(), calls=%async_computation.20 | async-start | bytes 9437184 | tf_op jit(solution)/shard_map/reduce_scatter | solution.py:221
  884.9 21.7 %copy-start.14 = (bf16[1024,2,192]{0,2,1:T(8,128)(2,1)S(1)}, bf16[1024,2,192]{0,2,1:T(8,128)(2,1)}, u32[]{:S(2)}) copy-start(bf16[1024,2,192]{0,2,1:T(8,128)(2,1)} %copy-done.13) | copy-start | bytes 2359300
  892.2 2.3 copy-start.6
  894.6 1.2 copy-start.7
  903.1 2.3 copy-start.6
  905.4 1.2 copy-start.7
  913.6 1.4 copy-start.8
  913.6 192.9 %reduce-scatter.31.cloned.1.call-start = ((), (), s32[]{:S(2)}) async-start(), calls=%async_computation.26 | async-start | bytes 81920
  916.2 209.3 %reduce-scatter.27.cloned.1.call-start = ((), (), s32[]{:S(2)}) async-start(), calls=%async_computation.24 | async-start | bytes 2621440 | tf_op jit(solution)/shard_map/reduce_scatter | solution.py:248
  923.3 7.5 copy-start.11
  923.3 226.6 %reduce-scatter.29.cloned.1.call-start = ((), (), s32[]{:S(2)}) async-start(), calls=%async_computation.25 | async-start | bytes 2621440 | tf_op jit(solution)/shard_map/reduce_scatter | solution.py:250
  930.7 243.8 %reduce-scatter.25.cloned.1.call-start = ((), (), s32[]{:S(2)}) async-start(), calls=%async_computation.23 | async-start | bytes 655360 | tf_op jit(solution)/shard_map/reduce_scatter | solution.py:246
  935.3 270.3 %reduce-scatter.23.cloned.1.call-start = ((), (), s32[]{:S(2)}) async-start(), calls=%async_computation.22 | async-start | bytes 1966080 | tf_op jit(solution)/shard_map/reduce_scatter | solution.py:244
  935.3 2.2 copy-start.26
  937.5 122.3 %copy-start.1 = (bf16[2,128,1024]{2,1,0:T(8,128)(2,1)S(1)}, bf16[2,128,1024]{2,1,0:T(8,128)(2,1)}, u32[]{:S(2)}) copy-start(bf16[2,128,1024]{2,1,0:T(8,128)(2,1)} %param.17) | copy-start | bytes 1572868
  937.5 122.3 %copy-start.17 = (f32[2,1024]{1,0:T(2,128)S(1)}, f32[2,1024]{1,0:T(2,128)}, u32[]{:S(2)}) copy-start(f32[2,1024]{1,0:T(2,128)} %copy-done.16) | copy-start | bytes 24580
  937.5 122.3 %copy-start.20 = (f32[2,128]{1,0:T(2,128)S(1)}, f32[2,128]{1,0:T(2,128)}, u32[]{:S(2)}) copy-start(f32[2,128]{1,0:T(2,128)} %copy-done.19) | copy-start | bytes 3076
  937.5 122.3 %copy-start.22 = (f32[2,128]{1,0:T(2,128)S(1)}, f32[2,128]{1,0:T(2,128)}, u32[]{:S(2)}) copy-start(f32[2,128]{1,0:T(2,128)} %copy-done.21) | copy-start | bytes 3076
  937.5 160.0 %copy-start.23 = (f32[2,128]{1,0:T(2,128)S(1)}, f32[2,128]{1,0:T(2,128)}, u32[]{:S(2)}) copy-start(f32[2,128]{1,0:T(2,128)} %param.19) | copy-start | bytes 3076
  940.5 159.3 %copy-start.30 = (u32[32]{0:T(128)S(1)}, u32[32]{0:T(128)}, u32[]{:S(2)}) copy-start(u32[32]{0:T(128)} %constant.80) | copy-start | bytes 388
  940.6 305.7 %reduce-scatter.21.cloned.1.call-start = ((), (), s32[]{:S(2)}) async-start(), calls=%async_computation.21 | async-start | bytes 3932160 | tf_op jit(solution)/shard_map/reduce_scatter | solution.py:242
  1102.4 3.5 copy-start.2
  1102.4 19.4 %copy-start.5 = (bf16[128,6144]{1,0:T(8,128)(2,1)S(1)}, bf16[128,6144]{1,0:T(8,128)(2,1)}, u32[]{:S(2)}) copy-start(bf16[128,6144]{1,0:T(8,128)(2,1)} %all-gather.13.cloned.1.call-done) | copy-start | bytes 4718596
  1102.4 20.5 %copy-start.4 = (f32[2,128,1024]{2,1,0:T(8,128)S(1)}, f32[2,128,1024]{2,1,0:T(8,128)}, u32[]{:S(2)}) copy-start(f32[2,128,1024]{2,1,0:T(8,128)} %copy-done.3) | copy-start | bytes 3145732
Sparse Core Ops, SparseCore 0:
  9.6 22.3 all-gather.12
  74.2 69.0 all-gather.14
  160.7 145.9 reduce-scatter.12
  308.1 15.7 all-gather.18
  326.6 72.7 all-gather.16
  400.8 15.3 all-gather.20
  418.9 72.7 all-gather.22
  506.5 145.9 reduce-scatter.16
  656.2 146.5 reduce-scatter.14
  808.4 71.8 all-gather.24
  913.8 145.9 reduce-scatter.18
  1062.1 18.6 reduce-scatter.30
  1083.9 31.3 reduce-scatter.26
  1118.3 31.5 reduce-scatter.28
  1152.8 21.6 reduce-scatter.24
  1177.4 28.0 reduce-scatter.22
  1208.5 37.7 reduce-scatter.20
where the time goes:
time: 1260 us; the launch traced here: 1250 us
  waiting for transfers between devices  966 us (77%)
  blocking collectives  126 us (10%)
  matrix products  94.7 us (8%)
  other arithmetic  32.1 us (3%)
  between operations  16.6 us (1%)
  local copies, waits for them, and re-layouts  16.5 us (1%)
    reduce_scatter x1, waiting for transfers between devices, on_device(): lax.psum_scatter(mlp_terms, 'tp', scatter_dimension=1, tiled=True)  148 us
    reduce_scatter x1, waiting for transfers between devices, on_device(): lax.psum_scatter(attn_terms, 'tp', scatter_dimension=1, tiled=True)  140 us
    reduce_scatter x1, waiting for transfers between devices, on_device(): lax.psum_scatter(mlp_in_terms, 'tp', scatter_dimension=1, tiled=True)  132 us
    reduce_scatter x1, waiting for transfers between devices, on_device(): lax.psum_scatter(attn_in_terms, 'tp', scatter_dimension=1, tiled=True)  119 us
    all_gather x1, waiting for transfers between devices, on_device(): lax.all_gather(grad_mlp_out, 'tp', axis=1, tiled=True)  75.6 us
    all_gather x1, waiting for transfers between devices, on_device(): mlp_rows = lax.all_gather(mlp_local, 'tp', axis=1, tiled=True)  75.4 us
    all_gather x1, waiting for transfers between devices, on_device(): lax.all_gather(grad_attn_out, 'tp', axis=1, tiled=True)  72 us
    all_gather x1, waiting for transfers between devices, on_device(): attn_rows = lax.all_gather(attn_local, 'tp', axis=1, tiled=True)  49.3 us
  transfers between devices with their start and end apart: 17, of which 15 were waited for; matrix products, arithmetic and copies ran while one was open for 5% of the time, Pallas kernels for 0%

commit v1 on v0

--- a/solution.py
+++ b/solution.py
@@ -233,7 +233,11 @@
         ],
         -1,
     )
-    grad_modulation = lax.psum(mod_terms, "tp")
+    grad_modulation = mod_terms
+    for hop in (1, 2, 4):
+        grad_modulation = grad_modulation + lax.ppermute(
+            grad_modulation, "tp", [(dev, dev ^ hop) for dev in range(8)]
+        )
     grad_mod_low = grad_modulation.astype(jnp.bfloat16)
     grad_mod_w = jnp.dot(cond_low.T, grad_mod_low, preferred_element_type=jnp.float32)
     grad_mod_bias = jnp.sum(grad_modulation, 0)

time: 1260 us -> 1260 us (level)
  blocking collectives: 126 us -> 89.2 us
  waiting for transfers between devices: 966 us -> 998 us
    psum x1 -> x0, blocking collectives: 35.9 us -> none  [on_device(): grad_modulation = lax.psum(mod_terms, 'tp')]
  transfers between devices with their start and end apart: 17 -> 20, of which waited for: 15 -> 19; matrix products, arithmetic and copies ran while one was open for 5% -> 5% of each run, Pallas kernels for 0% -> 0%
where the time goes in v1:
time: 1260 us; the launch traced here: 1250 us
  waiting for transfers between devices  998 us (79%)
  matrix products  94.7 us (8%)
  blocking collectives  89.2 us (7%)
  other arithmetic  32.1 us (3%)
  between operations  16.6 us (1%)
  local copies, waits for them, and re-layouts  16.5 us (1%)
    reduce_scatter x1, waiting for transfers between devices, on_device(): lax.psum_scatter(mlp_terms, 'tp', scatter_dimension=1, tiled=True)  148 us
    reduce_scatter x1, waiting for transfers between devices, on_device(): lax.psum_scatter(attn_terms, 'tp', scatter_dimension=1, tiled=True)  140 us
    reduce_scatter x1, waiting for transfers between devices, on_device(): lax.psum_scatter(mlp_in_terms, 'tp', scatter_dimension=1, tiled=True)  132 us
    reduce_scatter x1, waiting for transfers between devices, on_device(): lax.psum_scatter(attn_in_terms, 'tp', scatter_dimension=1, tiled=True)  119 us
    all_gather x1, waiting for transfers between devices, on_device(): lax.all_gather(grad_mlp_out, 'tp', axis=1, tiled=True)  75.6 us
    all_gather x1, waiting for transfers between devices, on_device(): mlp_rows = lax.all_gather(mlp_local, 'tp', axis=1, tiled=True)  75.4 us
    all_gather x1, waiting for transfers between devices, on_device(): lax.all_gather(grad_attn_out, 'tp', axis=1, tiled=True)  72 us
    all_gather x1, waiting for transfers between devices, on_device(): attn_rows = lax.all_gather(attn_local, 'tp', axis=1, tiled=True)  49.3 us
  transfers between devices with their start and end apart: 20, of which 19 were waited for; matrix products, arithmetic and copies ran while one was open for 5% of the time, Pallas kernels for 0%

profile of v1, /device:TPU:0, one launch (start us, length us, event | category | flops | bytes accessed | tf_op | source)
XLA Modules:
  0.0 1252.4 jit_solution(18168867390697138303)
XLA Ops:
  8.7 6.2 all-gather
  17.5 14.5 %all-gather.13.cloned.1.call-done = bf16[128,6144]{1,0:T(8,128)(2,1)} async-done(((bf16[128,1536]{1,0:T(8,128)(2,1)}), bf16[128,6144]{1,0:T(8,128)(2,1)}) %all-gather.13.cloned.1.call-update) | async-done | bytes 1572880 | tf_op jit(solution)/shard_map/all_gather | solution.py:104
  32.0 1.7 fusion.83
  33.7 37.5 %psum.7 = f32[2,6144]{1,0:T(2,128)S(1)} all-reduce(f32[2,6144]{1,0:T(2,128)S(1)} %fusion.83), channel_id=1, replica_groups=mesh['fsdp'=4,'tp'=8] {'tp'}, use_global_device_ids=true, to_apply=%region_0.1 | all-reduce | flops 12288 | bytes 98304 | tf_op jit(solution)/shard_map/psum | solution.py:119
  71.9 2.1 fusion.67
  74.1 5.1 all-gather.1
  79.4 5.8 all_gather.47
  85.3 8.7 all_gather.45
  94.0 49.3 %all-gather.15.cloned.1.call-done = bf16[2,1024,1024]{2,1,0:T(8,128)(2,1)} async-done(((bf16[2,128,1024]{2,1,0:T(8,128)(2,1)}), bf16[2,1024,1024]{2,1,0:T(8,128)(2,1)}) %all-gather.15.cloned.1.call-update) | async-done | bytes 4194320 | tf_op jit(solution)/shard_map/all_gather | solution.py:131
  143.3 4.0 add_convert_fusion
  147.5 8.6 while.22
  150.2 1.5 fusion.136
  154.5 1.5 fusion.136
  156.0 4.5 fusion.78
  161.2 5.1 all-gather.2
  166.3 140.4 %reduce-scatter.13.cloned.1.call-done = f32[2,128,1024]{2,1,0:T(8,128)} async-done(((f32[2,1024,1024]{2,1,0:T(8,128)}), f32[2,128,1024]{2,1,0:T(8,128)}) %reduce-scatter.13.cloned.1.call-update) | async-done | bytes 1048592 | tf_op jit(solution)/shard_map/reduce_scatter | solution.py:158
  306.7 1.5 fusion.87
  310.2 2.0 fusion.74
  312.2 5.2 all-gather.3
  317.5 6.5 all-gather.19.cloned.1.call-done
  324.0 75.4 %all-gather.17.cloned.1.call-done = bf16[2,1024,1024]{2,1,0:T(8,128)(2,1)} async-done(((bf16[2,128,1024]{2,1,0:T(8,128)(2,1)}), bf16[2,1024,1024]{2,1,0:T(8,128)(2,1)}) %all-gather.17.cloned.1.call-update) | async-done | bytes 4194320 | tf_op jit(solution)/shard_map/all_gather | solution.py:163
  399.4 6.8 fusion.92
  406.1 10.0 all-gather.21.cloned.1.call-done
  416.2 75.6 %all-gather.23.cloned.1.call-done = bf16[2,1024,1024]{2,1,0:T(8,128)(2,1)} async-done(((bf16[2,128,1024]{2,1,0:T(8,128)(2,1)}), bf16[2,1024,1024]{2,1,0:T(8,128)(2,1)}) %all-gather.23.cloned.1.call-update) | async-done | bytes 4194320 | tf_op jit(solution)/shard_map/all_gather | solution.py:179
  491.7 9.0 convert_reduce_fusion.2
  500.7 5.6 fusion.93
  506.4 8.6 fusion.85
  515.6 5.1 all-gather.4
  520.7 131.8 %reduce-scatter.17.cloned.1.call-done = f32[2,128,1024]{2,1,0:T(8,128)} async-done(((f32[2,1024,1024]{2,1,0:T(8,128)}), f32[2,128,1024]{2,1,0:T(8,128)}) %reduce-scatter.17.cloned.1.call-update) | async-done | bytes 1048592 | tf_op jit(solution)/shard_map/reduce_scatter | solution.py:193
  652.5 1.7 multiply_reduce_fusion.2
  654.3 148.5 %reduce-scatter.15.cloned.1.call-done = f32[2,128,1024]{2,1,0:T(8,128)} async-done(((f32[2,1024,1024]{2,1,0:T(8,128)}), f32[2,128,1024]{2,1,0:T(8,128)}) %reduce-scatter.15.cloned.1.call-update) | async-done | bytes 1048592 | tf_op jit(solution)/shard_map/reduce_scatter | solution.py:172
  802.8 3.6 fusion.75
  808.3 72.0 %all-gather.25.cloned.1.call-done = bf16[2,1024,1024]{2,1,0:T(8,128)(2,1)} async-done(((bf16[2,128,1024]{2,1,0:T(8,128)(2,1)}), bf16[2,1024,1024]{2,1,0:T(8,128)(2,1)}) %all-gather.25.cloned.1.call-update) | async-done | bytes 4194320 | tf_op jit(solution)/shard_map/all_gather | solution.py:199
  880.3 3.4 convolution_convert_fusion
  884.9 21.7 %while.23 = (s32[]{:T(128)}, bf16[2,1024,2,192]{1,3,2,0:T(8,128)(2,1)}, bf16[2,1024,2,64]{1,3,2,0:T(8,128)(2,1)S(1)}, bf16[2,1024,2,64]{1,3,2,0:T(8,128)(2,1)S(1...) while((s32[]{:T(128)}, ...), condition=%wide.region_16.17_spmd, body=%wide.region_14.16_spmd.sunk | while | flops 1370355712 | bytes 79751328 | solution.py:209
  886.2 1.6 fusion.146
  887.8 2.0 multiply_reduce_fusion.11
  889.8 2.4 multiply_convert_fusion.9
  893.1 1.4 fusion.147
  897.1 1.6 fusion.146
  898.6 2.0 multiply_reduce_fusion.11
  900.6 2.4 multiply_convert_fusion.9
  906.6 7.0 convolution_bitcast_fusion
  916.6 6.6 fusion.96
  923.3 7.3 fusion.84
  931.4 3.8 fusion.95
  935.3 1.6 copy.70
  937.5 3.0 fusion.94
  940.8 119.0 %reduce-scatter.19.cloned.1.call-done = f32[2,128,1024]{2,1,0:T(8,128)} async-done(((f32[2,1024,1024]{2,1,0:T(8,128)}), f32[2,128,1024]{2,1,0:T(8,128)}) %reduce-scatter.19.cloned.1.call-update) | async-done | bytes 1048592 | tf_op jit(solution)/shard_map/reduce_scatter | solution.py:221
  1059.8 1.8 fusion.72
  1061.7 1.5 collective-permute-start
  1063.2 2.6 collective-permute-done
  1066.4 3.6 collective-permute-done.1
  1070.0 1.9 collective-permute-start.2
  1071.9 3.6 collective-permute-done.2
  1075.6 2.3 fusion.82
  1080.5 3.0 convert_reduce_fusion
  1086.0 2.6 fusion.71
  1088.6 10.5 all-reduce.4
  1102.7 12.5 reduce-scatter.27.cloned.1.call-done
  1115.1 34.1 %reduce-scatter.29.cloned.1.call-done = f32[512,256]{1,0:T(8,128)} async-done(((f32[512,1024]{1,0:T(8,128)}), f32[512,256]{1,0:T(8,128)}) %reduce-scatter.29.cloned.1.call-update) | async-done | bytes 524304 | tf_op jit(solution)/shard_map/reduce_scatter | solution.py:254
  1149.3 24.6 %reduce-scatter.25.cloned.1.call-done = f32[128,256]{1,0:T(8,128)} async-done(((f32[128,1024]{1,0:T(8,128)}), f32[128,256]{1,0:T(8,128)}) %reduce-scatter.25.cloned.1.call-update) | async-done | bytes 131088 | tf_op jit(solution)/shard_map/reduce_scatter | solution.py:250
  1173.8 31.1 %reduce-scatter.23.cloned.1.call-done = f32[256,2,192]{0,2,1:T(8,128)} async-done(((f32[1024,2,192]{0,2,1:T(8,128)}), f32[256,2,192]{0,2,1:T(8,128)}) %reduce-scatter.23.cloned.1.call-update) | async-done | bytes 393232 | tf_op jit(solution)/shard_map/reduce_scatter | solution.py:248
  1204.9 40.8 %reduce-scatter.21.cloned.1.call-done = f32[128,1536]{1,0:T(8,128)} async-done(((f32[128,6144]{1,0:T(8,128)}), f32[128,1536]{1,0:T(8,128)}) %reduce-scatter.21.cloned.1.call-update) | async-done | bytes 786448 | tf_op jit(solution)/shard_map/reduce_scatter | solution.py:246
  (174 shorter events, 37.2 us)
Async XLA Ops:
  7.2 67.0 %copy-start.24 = (bf16[2,32]{1,0:T(2,128)(2,1)S(1)}, bf16[2,32]{1,0:T(2,128)(2,1)}, u32[]{:S(2)}) copy-start(bf16[2,32]{1,0:T(2,128)(2,1)} %param.23) | copy-start | bytes 388
  7.2 72.2 %copy-start.18 = (bf16[128,256]{1,0:T(8,128)(2,1)S(1)}, bf16[128,256]{1,0:T(8,128)(2,1)}, u32[]{:S(2)}) copy-start(bf16[128,256]{1,0:T(8,128)(2,1)} %param.24) | copy-start | bytes 196612
  7.2 78.1 %copy-start.15 = (bf16[256,2,192]{0,2,1:T(8,128)(2,1)S(1)}, bf16[256,2,192]{0,2,1:T(8,128)(2,1)}, u32[]{:S(2)}) copy-start(bf16[256,2,192]{0,2,1:T(8,128)(2,1)} %param.22) | copy-start | bytes 589828
  7.2 24.8 %all-gather.13.cloned.1.call-start = ((), (), s32[]{:S(2)}) async-start(), calls=%async_computation.10 | async-start | bytes 1966080 | tf_op jit(solution)/shard_map/all_gather | solution.py:104
  7.9 135.4 %all-gather.15.cloned.1.call-start = ((), (), s32[]{:S(2)}) async-start(), calls=%async_computation.11 | async-start | bytes 4718592 | tf_op jit(solution)/shard_map/all_gather | solution.py:131
  16.1 131.2 %copy-start.19 = (f32[2,128]{1,0:T(2,128)}, f32[2,128]{1,0:T(2,128)S(1)}, u32[]{:S(2)}) copy-start(f32[2,128]{1,0:T(2,128)S(1)} %broadcast_multiply_fusion.5) | copy-start | bytes 3076
  17.5 56.6 %copy-start.21 = (f32[2,128]{1,0:T(2,128)}, f32[2,128]{1,0:T(2,128)S(1)}, u32[]{:S(2)}) copy-start(f32[2,128]{1,0:T(2,128)S(1)} %add_rsqrt_fusion.1) | copy-start | bytes 3076
  71.3 0.6 copy-start.16
  74.1 232.7 %reduce-scatter.13.cloned.1.call-start = ((), (), s32[]{:S(2)}) async-start(), calls=%async_computation.12 | async-start | bytes 9437184 | tf_op jit(solution)/shard_map/reduce_scatter | solution.py:158
  94.0 53.3 %copy-start.13 = (bf16[1024,2,192]{0,2,1:T(8,128)(2,1)}, bf16[1024,2,192]{0,2,1:T(8,128)(2,1)S(1)}, u32[]{:S(2)}) copy-start(bf16[1024,2,192]{0,2,1:T(8,128)(2,1)S(1)} %all_gather.45) | copy-start | bytes 2359300
  156.0 4.5 copy-start.10
  160.6 0.7 copy-start.28
  160.6 146.2 %copy-start = (bf16[2,128,1024]{2,1,0:T(8,128)(2,1)S(1)}, bf16[2,128,1024]{2,1,0:T(8,128)(2,1)}, u32[]{:S(2)}) copy-start(bf16[2,128,1024]{2,1,0:T(8,128)(2,1)} %param.17) | copy-start | bytes 1572868
  160.6 151.7 %copy-start.25 = (bf16[128]{0:T(256)(128)(2,1)S(1)}, bf16[128]{0:T(256)(128)(2,1)}, u32[]{:S(2)}) copy-start(bf16[128]{0:T(256)(128)(2,1)} %param.27) | copy-start | bytes 772
  160.6 163.4 %all-gather.19.cloned.1.call-start = ((), (), s32[]{:S(2)}) async-start(), calls=%async_computation.14 | async-start | bytes 1310720 | tf_op jit(solution)/shard_map/all_gather | solution.py:110
  161.2 238.2 %all-gather.17.cloned.1.call-start = ((), (), s32[]{:S(2)}) async-start(), calls=%async_computation.13 | async-start | bytes 4718592 | tf_op jit(solution)/shard_map/all_gather | solution.py:163
  309.6 106.6 %all-gather.21.cloned.1.call-start = ((), (), s32[]{:S(2)}) async-start(), calls=%async_computation.15 | async-start | bytes 1310720 | tf_op jit(solution)/shard_map/all_gather | solution.py:112
  310.2 181.6 %all-gather.23.cloned.1.call-start = ((), (), s32[]{:S(2)}) async-start(), calls=%async_computation.17 | async-start | bytes 4718592 | tf_op jit(solution)/shard_map/all_gather | solution.py:179
  312.2 340.3 %reduce-scatter.17.cloned.1.call-start = ((), (), s32[]{:S(2)}) async-start(), calls=%async_computation.18 | async-start | bytes 9437184 | tf_op jit(solution)/shard_map/reduce_scatter | solution.py:193
  491.7 9.0 copy-start.27
  500.7 5.6 copy-start.12
  506.4 296.4 %reduce-scatter.15.cloned.1.call-start = ((), (), s32[]{:S(2)}) async-start(), calls=%async_computation.16 | async-start | bytes 9437184 | tf_op jit(solution)/shard_map/reduce_scatter | solution.py:172
  515.0 0.7 copy-start.29
  515.0 287.8 %copy-start.9 = (bf16[2,128,1024]{2,1,0:T(8,128)(2,1)S(1)}, bf16[2,128,1024]{2,1,0:T(8,128)(2,1)}, u32[]{:S(2)}) copy-start(bf16[2,128,1024]{2,1,0:T(8,128)(2,1)} %param.18) | copy-start | bytes 1572868
  515.0 365.3 %all-gather.25.cloned.1.call-start = ((), (), s32[]{:S(2)}) async-start(), calls=%async_computation.19 | async-start | bytes 4718592 | tf_op jit(solution)/shard_map/all_gather | solution.py:199
  806.4 1.0 copy-start.3
  808.3 251.5 %reduce-scatter.19.cloned.1.call-start = ((), (), s32[]{:S(2)}) async-start(), calls=%async_computation.20 | async-start | bytes 9437184 | tf_op jit(solution)/shard_map/reduce_scatter | solution.py:221
  884.9 21.7 %copy-start.14 = (bf16[1024,2,192]{0,2,1:T(8,128)(2,1)S(1)}, bf16[1024,2,192]{0,2,1:T(8,128)(2,1)}, u32[]{:S(2)}) copy-start(bf16[1024,2,192]{0,2,1:T(8,128)(2,1)} %copy-done.13) | copy-start | bytes 2359300
  892.2 2.3 copy-start.6
  894.6 1.2 copy-start.7
  903.1 2.3 copy-start.6
  905.4 1.2 copy-start.7
  913.6 1.4 copy-start.8
  913.6 171.0 %reduce-scatter.31.cloned.1.call-start = ((), (), s32[]{:S(2)}) async-start(), calls=%async_computation.26 | async-start | bytes 81920
  916.2 199.0 %reduce-scatter.27.cloned.1.call-start = ((), (), s32[]{:S(2)}) async-start(), calls=%async_computation.24 | async-start | bytes 2621440 | tf_op jit(solution)/shard_map/reduce_scatter | solution.py:252
  923.3 7.5 copy-start.11
  923.3 226.0 %reduce-scatter.29.cloned.1.call-start = ((), (), s32[]{:S(2)}) async-start(), calls=%async_computation.25 | async-start | bytes 2621440 | tf_op jit(solution)/shard_map/reduce_scatter | solution.py:254
  930.7 243.2 %reduce-scatter.25.cloned.1.call-start = ((), (), s32[]{:S(2)}) async-start(), calls=%async_computation.23 | async-start | bytes 655360 | tf_op jit(solution)/shard_map/reduce_scatter | solution.py:250
  935.2 269.7 %reduce-scatter.23.cloned.1.call-start = ((), (), s32[]{:S(2)}) async-start(), calls=%async_computation.22 | async-start | bytes 1966080 | tf_op jit(solution)/shard_map/reduce_scatter | solution.py:248
  935.3 2.2 copy-start.26
  937.5 122.3 %copy-start.1 = (bf16[2,128,1024]{2,1,0:T(8,128)(2,1)S(1)}, bf16[2,128,1024]{2,1,0:T(8,128)(2,1)}, u32[]{:S(2)}) copy-start(bf16[2,128,1024]{2,1,0:T(8,128)(2,1)} %param.17) | copy-start | bytes 1572868
  937.5 122.3 %copy-start.17 = (f32[2,1024]{1,0:T(2,128)S(1)}, f32[2,1024]{1,0:T(2,128)}, u32[]{:S(2)}) copy-start(f32[2,1024]{1,0:T(2,128)} %copy-done.16) | copy-start | bytes 24580
  937.5 122.3 %copy-start.20 = (f32[2,128]{1,0:T(2,128)S(1)}, f32[2,128]{1,0:T(2,128)}, u32[]{:S(2)}) copy-start(f32[2,128]{1,0:T(2,128)} %copy-done.19) | copy-start | bytes 3076
  937.5 122.3 %copy-start.22 = (f32[2,128]{1,0:T(2,128)S(1)}, f32[2,128]{1,0:T(2,128)}, u32[]{:S(2)}) copy-start(f32[2,128]{1,0:T(2,128)} %copy-done.21) | copy-start | bytes 3076
  937.5 138.1 %copy-start.23 = (f32[2,128]{1,0:T(2,128)S(1)}, f32[2,128]{1,0:T(2,128)}, u32[]{:S(2)}) copy-start(f32[2,128]{1,0:T(2,128)} %param.19) | copy-start | bytes 3076
  940.5 137.4 %copy-start.30 = (u32[32]{0:T(128)S(1)}, u32[32]{0:T(128)}, u32[]{:S(2)}) copy-start(u32[32]{0:T(128)} %constant.80) | copy-start | bytes 388
  940.6 305.1 %reduce-scatter.21.cloned.1.call-start = ((), (), s32[]{:S(2)}) async-start(), calls=%async_computation.21 | async-start | bytes 3932160 | tf_op jit(solution)/shard_map/reduce_scatter | solution.py:246
  1061.7 4.2 collective-permute-start
  1065.8 4.2 collective-permute-start.1
  1070.0 5.5 collective-permute-start.2
  1080.5 3.5 copy-start.2
  1080.5 5.5 copy-start.4
  1083.9 17.7 %copy-start.5 = (bf16[128,6144]{1,0:T(8,128)(2,1)S(1)}, bf16[128,6144]{1,0:T(8,128)(2,1)}, u32[]{:S(2)}) copy-start(bf16[128,6144]{1,0:T(8,128)(2,1)} %all-gather.13.cloned.1.call-done) | copy-start | bytes 4718596
Sparse Core Ops, SparseCore 0:
  9.6 22.3 all-gather.12
  74.2 69.0 all-gather.14
  160.7 145.9 reduce-scatter.12
  308.1 15.7 all-gather.18
  326.6 72.7 all-gather.16
  400.8 15.3 all-gather.20
  418.9 72.7 all-gather.22
  506.5 145.9 reduce-scatter.16
  656.2 146.5 reduce-scatter.14
  808.4 71.8 all-gather.24
  913.8 145.9 reduce-scatter.18
  1062.1 18.6 reduce-scatter.30
  1083.9 31.2 reduce-scatter.26
  1118.1 31.1 reduce-scatter.28
  1152.2 21.6 reduce-scatter.24
  1176.8 28.0 reduce-scatter.22
  1207.9 37.7 reduce-scatter.20
